TPU v7x, 256 devices: a whole 4x4x8 slice. The times are simulated.
256 devices in a mesh: trow: 4 (over y), tcol: 4 (over x), pix: 16 (over z, core).
Axes of the slice: x: 4, y: 4, z: 8, core: 2. Of those that a mesh axis runs over, the one named last changes fastest.
Arguments:
- frames: float32 [6144, 2, 64, 128], P(('trow', 'tcol'), None, 'pix'), may hold values from 0.1 to 8
- drift: int32 [6144, 2], P(('trow', 'tcol')), may hold values from -7 to 7
Outputs:
- inner_cycle: float32 [6144, 6144], P(('trow', 'pix'), 'tcol')
- second_band_twotime: float32 [6144, 6144], P(('trow', 'pix'), 'tcol')
All inputs are finite; a program needn't handle non-finite values.
Results may differ from a plain program's by a relative error of at most 0.0003.
Values may be sent and summed in bfloat16 or wider, within the bound.
A program may use at most 128 MiB of HBM per device.

v0:
```python
import jax
import jax.numpy as jnp
from jax import lax
from jax.sharding import PartitionSpec as P


def extended(cells, sides, width):
    for axis, dim in sides:
        count = lax.axis_size(axis)
        ends = count - 1
        head = lax.slice_in_dim(cells, 0, width, axis=dim)
        tail = lax.slice_in_dim(cells, cells.shape[dim] - width, cells.shape[dim], axis=dim)
        cells = jnp.concatenate(
            [
                lax.ppermute(tail, axis, [(i, (i + 1) % count) for i in range(ends)]),
                cells,
                lax.ppermute(head, axis, [((i + 1) % count, i) for i in range(ends)]),
            ],
            axis=dim,
        )
    return cells


def blend(padded, steps, device_axis):
    upward = (jnp.maximum(steps, 0).astype(jnp.float32) / 8.0)[:, None, None, None]
    downward = (jnp.maximum(-steps, 0).astype(jnp.float32) / 8.0)[:, None, None, None]
    length = padded.shape[device_axis] - 2
    middle = lax.slice_in_dim(padded, 1, 1 + length, 1, device_axis)
    after = lax.slice_in_dim(padded, 2, 2 + length, 1, device_axis)
    before = lax.slice_in_dim(padded, 0, length, 1, device_axis)
    return (1.0 - upward - downward) * middle + upward * after + downward * before


def per_device(frames, drift):
    local_frames = frames.shape[0]
    tile_rows = frames.shape[2]
    columns = frames.shape[3]
    total_frames = local_frames * lax.axis_size("trow") * lax.axis_size("tcol")
    band_pixels = tile_rows * columns * lax.axis_size("pix")
    padded = extended(frames.astype(jnp.bfloat16), (("pix", 2),), 1).astype(frames.dtype)
    rowpass = blend(padded, drift[:, 0], 2)
    padded = jnp.pad(rowpass, ((0, 0), (0, 0), (0, 0), (1, 1)))
    shifted = blend(padded, drift[:, 1], 3)
    pixel_mean = lax.psum(jnp.sum(shifted, axis=0), ("trow", "tcol")) / total_frames
    flat = shifted / pixel_mean[None]
    frame_mean = lax.psum(jnp.sum(flat, axis=(2, 3)), "pix") / band_pixels
    normed = (flat / frame_mean[:, :, None, None]).astype(jnp.bfloat16)
    normed = normed.reshape(local_frames, 2, tile_rows * columns)
    block_size = local_frames * lax.axis_size("tcol")
    everything = lax.all_gather(normed, ("trow", "tcol"), axis=0, tiled=True)
    row_frames = lax.dynamic_slice_in_dim(
        everything, lax.axis_index("trow") * block_size, block_size, 0
    )
    col_frames = lax.dynamic_slice_in_dim(
        everything, lax.axis_index("tcol") * block_size, block_size, 0
    )
    own_rows = block_size // lax.axis_size("pix")
    results = []
    for band in range(2):
        band_rows = row_frames[:, band]
        band_cols = col_frames[:, band]

        def partial_gram(start, count, band_rows=band_rows, band_cols=band_cols):
            return lax.dot_general(
                band_rows, band_cols, (((1,), (1,)), ((), ())), preferred_element_type=jnp.float32
            )

        summed = lax.psum_scatter(
            partial_gram(jnp.int32(0), lax.axis_size("pix") * own_rows),
            "pix",
            scatter_dimension=0,
            tiled=True,
        )
        results.append(summed / band_pixels)
    return (results[0], results[1])


def solution(mesh):
    in_specs = (P(("trow", "tcol"), None, "pix", None), P(("trow", "tcol"), None))
    out_specs = (P(("trow", "pix"), "tcol"), P(("trow", "pix"), "tcol"))
    return jax.shard_map(
        per_device, mesh=mesh, in_specs=in_specs, out_specs=out_specs, check_vma=False
    )
```

profile of v0, /device:TPU:6, one launch (start us, length us, event | category | flops | bytes accessed | tf_op | source)
XLA Modules:
  0.0 343.2 jit_solution(5031230959455782191)
XLA Ops:
  7.2 0.0 copy-start
  7.2 0.0 all-gather.2.cloned.1.call-start
  7.2 1.7 copy.10
  9.0 1.8 collective-permute-start
  10.7 1.3 collective-permute-start.1
  12.0 0.0 copy-done
  12.1 0.0 collective-permute-done
  12.1 3.7 %collective-permute-done.1 = bf16[384,2,1,128]{3,0,2,1:T(8,128)(2,1)S(1)} collective-permute-done((bf16[384,2,1,128]{3,0,2,1:T(8,128)(2,1)S(1)}, bf16[384,2,1,128]{3,0,2,1:T(8,128)(2,1)S(1)}, u32[]{:S(2)}, u32[]{:S(2)}) %collective-permute-start.1) | collective-permute-done | bytes 196640 | tf_op jit(solution)/shard_map/ppermute | solution.py:17
  15.8 0.2 maximum_convert_fusion
  15.9 0.4 fusion.6
  16.3 1.0 fusion.11
  17.4 32.7 %psum.14 = f32[2,4,128]{2,1,0:T(4,128)S(1)} all-reduce(f32[2,4,128]{2,1,0:T(4,128)S(1)} %get-tuple-element.6), channel_id=1, replica_groups=mesh['trow'=4,'tcol'=4,'pix'=16] {'trow','tcol'}, use_global_device_ids=true, to_apply=%region_1.2 | all-reduce | flops 1024 | bytes 8192 | tf_op jit(solution)/shard_map/psum | solution.py:44
  50.1 0.2 divide_reduce_fusion
  50.3 28.0 %psum.15 = f32[384,2]{0,1:T(2,128)S(1)} all-reduce(f32[384,2]{0,1:T(2,128)S(1)} %divide_reduce_fusion), channel_id=1, replica_groups=mesh['trow'=4,'tcol'=4,'pix'=16] {'pix'}, use_global_device_ids=true, to_apply=%region_3.4 | all-reduce | flops 768 | bytes 6144 | tf_op jit(solution)/shard_map/psum | solution.py:46
  78.3 1.2 copy_bitcast_fusion
  79.5 0.0 all-gather.2.cloned.1.call-update
  79.5 0.0 reduce-scatter.5.cloned.1.call-start
  79.6 99.5 %all-gather.2.cloned.1.call-done = bf16[6144,2,512]{2,0,1:T(8,128)(2,1)} async-done(((bf16[384,2,512]{2,0,1:T(8,128)(2,1)}), bf16[6144,2,512]{2,0,1:T(8,128)(2,1)}) %all-gather.2.cloned.1.call-update) | async-done | bytes 12582928 | tf_op jit(solution)/shard_map/all_gather | solution.py:50
  179.1 8.2 %fusion.4 = f32[1536,1536]{1,0:T(8,128)} fusion(bf16[6144,2,512]{2,0,1:T(8,128)(2,1)} %all-gather.2.cloned.1.call-done, s32[]{:T(128)S(6)} %select_n.7, s32[]{:T(128)S(6)} %add.38, s32[]{:T(128)S(6)} %select_n.6), kind=kOutput, calls=%fused_computation.7 | convolution fusion | flops 2415919104 | bytes 12584960 | tf_op jit(solution)/shard_map/dot_general | solution.py:64
  187.3 0.0 reduce-scatter.5.cloned.1.call-update
  187.3 0.0 reduce-scatter.3.cloned.1.call-start
  187.4 8.1 %fusion.5 = f32[1536,1536]{1,0:T(8,128)} fusion(bf16[6144,2,512]{2,0,1:T(8,128)(2,1)} %all-gather.2.cloned.1.call-done, s32[]{:T(128)S(6)} %select_n.7, s32[]{:T(128)S(6)} %select_n.6), kind=kOutput, calls=%fused_computation.10 | convolution fusion | flops 2415919104 | bytes 12582920 | tf_op jit(solution)/shard_map/dot_general | solution.py:64
  195.5 0.0 reduce-scatter.3.cloned.1.call-update
  195.5 64.3 %reduce-scatter.5.cloned.1.call-done = f32[96,1536]{1,0:T(8,128)} async-done(((f32[1536,1536]{1,0:T(8,128)}), f32[96,1536]{1,0:T(8,128)}) %reduce-scatter.5.cloned.1.call-update) | async-done | bytes 589840 | tf_op jit(solution)/shard_map/reduce_scatter | solution.py:68
  259.8 1.9 broadcast_multiply_fusion
  261.7 73.0 %reduce-scatter.3.cloned.1.call-done = f32[96,1536]{1,0:T(8,128)} async-done(((f32[1536,1536]{1,0:T(8,128)}), f32[96,1536]{1,0:T(8,128)}) %reduce-scatter.3.cloned.1.call-update) | async-done | bytes 589840 | tf_op jit(solution)/shard_map/reduce_scatter | solution.py:68
  334.7 1.9 broadcast_multiply_fusion.1
  (5 shorter events, 0.1 us)
Async XLA Ops:
  7.2 4.9 %copy-start = (s32[384,2]{0,1:T(2,128)S(1)}, s32[384,2]{0,1:T(2,128)}, u32[]{:S(2)}) copy-start(s32[384,2]{0,1:T(2,128)} %param.3) | copy-start | bytes 9220
  7.2 172.0 %all-gather.2.cloned.1.call-start = ((), (), s32[]{:S(2)}) async-start(), calls=%async_computation.2 | async-start | bytes 13369344 | tf_op jit(solution)/shard_map/all_gather | solution.py:50
  9.0 3.1 collective-permute-start
  10.7 5.0 %collective-permute-start.1 = (bf16[384,2,1,128]{3,0,2,1:T(8,128)(2,1)S(1)}, bf16[384,2,1,128]{3,0,2,1:T(8,128)(2,1)S(1)}, u32[]{:S(2)}, u32[]{:S(2)}) collective-permute-start(bf16[384,2,1,128]{3,0,2,1:T(8,128)(2,1)S(1)} %get-tuple-element.9), channel_id=1, source_target_pairs={{1,0},{2,1},{3,2},{4,3},{5,4},{6,5},{7,6},{8,7},{9,8},{10,9},{11,1... | collective-permute-start | bytes 589832 | tf_op jit(solution)/shard_map/ppermute | solution.py:17
  79.5 180.3 %reduce-scatter.5.cloned.1.call-start = ((), (), s32[]{:S(2)}) async-start(), calls=%async_computation.4 | async-start | bytes 10027008 | tf_op jit(solution)/shard_map/reduce_scatter | solution.py:68
  187.3 147.4 %reduce-scatter.3.cloned.1.call-start = ((), (), s32[]{:S(2)}) async-start(), calls=%async_computation.3 | async-start | bytes 10027008 | tf_op jit(solution)/shard_map/reduce_scatter | solution.py:68
Sparse Core Ops, SparseCore 0:
  79.7 99.4 all-gather.1
  187.5 72.3 reduce-scatter.4
  262.4 72.2 reduce-scatter.2
where the time goes:
time: 343 us
  waiting for transfers between devices  240 us (70%)
  blocking collectives  60.7 us (18%)
  matrix products  16.3 us (5%)
  between operations  13.8 us (4%)
  other arithmetic  6.9 us (2%)
    reduce_scatter x2, waiting for transfers between devices, per_device(): lax.psum_scatter(partial_gram(jnp.int32(0), lax.axis_size('pix') * own_ro...  137 us
    all_gather x1, waiting for transfers between devices, per_device(): everything = lax.all_gather(normed, ('trow', 'tcol'), axis=0, tiled=True)  99.5 us
    psum x1, blocking collectives, per_device(): lax.psum(jnp.sum(shifted, axis=0), ('trow', 'tcol')) / total_frames  32.7 us
    psum x1, blocking collectives, per_device(): frame_mean = lax.psum(jnp.sum(flat, axis=(2, 3)), 'pix') / band_pixels  28 us
    dot_general x2, matrix products, partial_gram(): lax.dot_general(band_rows, band_cols, (((1,), (1,)), ((), ())), preferred...  16.3 us
  transfers between devices with their start and end apart: 5, of which 4 were waited for; matrix products, arithmetic and copies ran while one was open for 3% of the time, Pallas kernels for 0%

commit v1 on v0

--- a/solution.py
+++ b/solution.py
@@ -41,7 +41,7 @@
     rowpass = blend(padded, drift[:, 0], 2)
     padded = jnp.pad(rowpass, ((0, 0), (0, 0), (0, 0), (1, 1)))
     shifted = blend(padded, drift[:, 1], 3)
-    pixel_mean = lax.psum(jnp.sum(shifted, axis=0), ("trow", "tcol")) / total_frames
+    pixel_mean = lax.psum(lax.psum(jnp.sum(shifted, axis=0), "trow"), "tcol") / total_frames
     flat = shifted / pixel_mean[None]
     frame_mean = lax.psum(jnp.sum(flat, axis=(2, 3)), "pix") / band_pixels
     normed = (flat / frame_mean[:, :, None, None]).astype(jnp.bfloat16)

time: 343 us -> 325 us (0.948)
  blocking collectives: 60.7 us -> 46.3 us
  waiting for transfers between devices: 240 us -> 236 us
    psum x1 -> x2, blocking collectives: 32.7 us -> 18.2 us  [the longest x1 10.8 us: per_device(): lax.psum(jnp.sum(shifted, axis=0), 'trow')]
    all_gather x1, waiting for transfers between devices: 99.5 us -> 95.2 us  [per_device(): everything = lax.all_gather(normed, ('trow', 'tcol'), axis=0, tiled=True)]
where the time goes in v1:
time: 325 us; the launch traced here: 324 us
  waiting for transfers between devices  236 us (73%)
  blocking collectives  46.3 us (14%)
  matrix products  16.3 us (5%)
  between operations  13.8 us (4%)
  other arithmetic  6.9 us (2%)
    reduce_scatter x2, waiting for transfers between devices, per_device(): lax.psum_scatter(partial_gram(jnp.int32(0), lax.axis_size('pix') * own_ro...  137 us
    all_gather x1, waiting for transfers between devices, per_device(): everything = lax.all_gather(normed, ('trow', 'tcol'), axis=0, tiled=True)  95.2 us
    psum x1, blocking collectives, per_device(): frame_mean = lax.psum(jnp.sum(flat, axis=(2, 3)), 'pix') / band_pixels  28 us
    dot_general x2, matrix products, partial_gram(): lax.dot_general(band_rows, band_cols, (((1,), (1,)), ((), ())), preferred...  16.3 us
    psum x1, blocking collectives, per_device(): lax.psum(jnp.sum(shifted, axis=0), 'trow')  10.8 us
    psum x1, blocking collectives, per_device(): lax.psum(lax.psum(jnp.sum(shifted, axis=0), 'trow'), 'tcol') / total_frames  7.47 us
  transfers between devices with their start and end apart: 5, of which 4 were waited for; matrix products, arithmetic and copies ran while one was open for 3% of the time, Pallas kernels for 0%

profile of v1, /device:TPU:6, one launch (start us, length us, event | category | flops | bytes accessed | tf_op | source)
XLA Modules:
  0.0 324.2 jit_solution(13328682774856160807)
XLA Ops:
  7.2 0.0 copy-start
  7.2 0.0 all-gather.2.cloned.1.call-start
  7.2 1.7 copy.10
  9.0 1.8 collective-permute-start
  10.7 1.3 collective-permute-start.1
  12.0 0.0 copy-done
  12.1 0.0 collective-permute-done
  12.1 3.7 %collective-permute-done.1 = bf16[384,2,1,128]{3,0,2,1:T(8,128)(2,1)S(1)} collective-permute-done((bf16[384,2,1,128]{3,0,2,1:T(8,128)(2,1)S(1)}, bf16[384,2,1,128]{3,0,2,1:T(8,128)(2,1)S(1)}, u32[]{:S(2)}, u32[]{:S(2)}) %collective-permute-start.1) | collective-permute-done | bytes 196640 | tf_op jit(solution)/shard_map/ppermute | solution.py:17
  15.8 0.2 maximum_convert_fusion
  15.9 0.4 fusion.6
  16.3 1.0 fusion.11
  17.4 10.8 %psum.21 = f32[2,4,128]{2,1,0:T(4,128)S(1)} all-reduce(f32[2,4,128]{2,1,0:T(4,128)S(1)} %get-tuple-element.6), channel_id=1, replica_groups=mesh['trow'=4,'tcol'=4,'pix'=16] {'trow'}, use_global_device_ids=true, to_apply=%region_1.2 | all-reduce | flops 1024 | bytes 8192 | tf_op jit(solution)/shard_map/psum | solution.py:44
  28.1 7.5 %psum.22 = f32[2,4,128]{2,1,0:T(4,128)S(1)} all-reduce(f32[2,4,128]{2,1,0:T(4,128)S(1)} %psum.21), channel_id=1, replica_groups=mesh['trow'=4,'tcol'=4,'pix'=16] {'tcol'}, use_global_device_ids=true, to_apply=%region_2.3 | all-reduce | flops 1024 | bytes 8192 | tf_op jit(solution)/shard_map/psum | solution.py:44
  35.6 0.2 divide_reduce_fusion
  35.8 28.0 %psum.23 = f32[384,2]{0,1:T(2,128)S(1)} all-reduce(f32[384,2]{0,1:T(2,128)S(1)} %divide_reduce_fusion), channel_id=1, replica_groups=mesh['trow'=4,'tcol'=4,'pix'=16] {'pix'}, use_global_device_ids=true, to_apply=%region_4.5 | all-reduce | flops 768 | bytes 6144 | tf_op jit(solution)/shard_map/psum | solution.py:46
  63.8 1.2 copy_bitcast_fusion
  65.0 0.0 all-gather.2.cloned.1.call-update
  65.1 0.0 reduce-scatter.5.cloned.1.call-start
  65.1 95.2 %all-gather.2.cloned.1.call-done = bf16[6144,2,512]{2,0,1:T(8,128)(2,1)} async-done(((bf16[384,2,512]{2,0,1:T(8,128)(2,1)}), bf16[6144,2,512]{2,0,1:T(8,128)(2,1)}) %all-gather.2.cloned.1.call-update) | async-done | bytes 12582928 | tf_op jit(solution)/shard_map/all_gather | solution.py:50
  160.3 8.2 %fusion.4 = f32[1536,1536]{1,0:T(8,128)} fusion(bf16[6144,2,512]{2,0,1:T(8,128)(2,1)} %all-gather.2.cloned.1.call-done, s32[]{:T(128)S(6)} %select_n.7, s32[]{:T(128)S(6)} %add.40, s32[]{:T(128)S(6)} %select_n.6), kind=kOutput, calls=%fused_computation.7 | convolution fusion | flops 2415919104 | bytes 12584960 | tf_op jit(solution)/shard_map/dot_general | solution.py:64
  168.5 0.0 reduce-scatter.5.cloned.1.call-update
  168.5 0.0 reduce-scatter.3.cloned.1.call-start
  168.6 8.1 %fusion.5 = f32[1536,1536]{1,0:T(8,128)} fusion(bf16[6144,2,512]{2,0,1:T(8,128)(2,1)} %all-gather.2.cloned.1.call-done, s32[]{:T(128)S(6)} %select_n.7, s32[]{:T(128)S(6)} %select_n.6), kind=kOutput, calls=%fused_computation.10 | convolution fusion | flops 2415919104 | bytes 12582920 | tf_op jit(solution)/shard_map/dot_general | solution.py:64
  176.7 0.0 reduce-scatter.3.cloned.1.call-update
  176.7 64.6 %reduce-scatter.5.cloned.1.call-done = f32[96,1536]{1,0:T(8,128)} async-done(((f32[1536,1536]{1,0:T(8,128)}), f32[96,1536]{1,0:T(8,128)}) %reduce-scatter.5.cloned.1.call-update) | async-done | bytes 589840 | tf_op jit(solution)/shard_map/reduce_scatter | solution.py:68
  241.3 1.9 broadcast_multiply_fusion
  243.2 72.5 %reduce-scatter.3.cloned.1.call-done = f32[96,1536]{1,0:T(8,128)} async-done(((f32[1536,1536]{1,0:T(8,128)}), f32[96,1536]{1,0:T(8,128)}) %reduce-scatter.3.cloned.1.call-update) | async-done | bytes 589840 | tf_op jit(solution)/shard_map/reduce_scatter | solution.py:68
  315.8 1.9 broadcast_multiply_fusion.1
  (5 shorter events, 0.1 us)
Async XLA Ops:
  7.2 4.9 %copy-start = (s32[384,2]{0,1:T(2,128)S(1)}, s32[384,2]{0,1:T(2,128)}, u32[]{:S(2)}) copy-start(s32[384,2]{0,1:T(2,128)} %param.3) | copy-start | bytes 9220
  7.2 153.1 %all-gather.2.cloned.1.call-start = ((), (), s32[]{:S(2)}) async-start(), calls=%async_computation.2 | async-start | bytes 13369344 | tf_op jit(solution)/shard_map/all_gather | solution.py:50
  9.0 3.1 collective-permute-start
  10.7 5.0 %collective-permute-start.1 = (bf16[384,2,1,128]{3,0,2,1:T(8,128)(2,1)S(1)}, bf16[384,2,1,128]{3,0,2,1:T(8,128)(2,1)S(1)}, u32[]{:S(2)}, u32[]{:S(2)}) collective-permute-start(bf16[384,2,1,128]{3,0,2,1:T(8,128)(2,1)S(1)} %get-tuple-element.9), channel_id=1, source_target_pairs={{1,0},{2,1},{3,2},{4,3},{5,4},{6,5},{7,6},{8,7},{9,8},{10,9},{11,1... | collective-permute-start | bytes 589832 | tf_op jit(solution)/shard_map/ppermute | solution.py:17
  65.1 176.2 %reduce-scatter.5.cloned.1.call-start = ((), (), s32[]{:S(2)}) async-start(), calls=%async_computation.4 | async-start | bytes 10027008 | tf_op jit(solution)/shard_map/reduce_scatter | solution.py:68
  168.5 147.3 %reduce-scatter.3.cloned.1.call-start = ((), (), s32[]{:S(2)}) async-start(), calls=%async_computation.3 | async-start | bytes 10027008 | tf_op jit(solution)/shard_map/reduce_scatter | solution.py:68
Sparse Core Ops, SparseCore 0:
  65.2 95.0 all-gather.1
  168.6 72.6 reduce-scatter.4
  243.9 71.8 reduce-scatter.2
